TPU v7x, 512 devices: a whole 4x4x16 slice. The times are simulated.
512 devices in a mesh: dp: 8 (over x, core), expert: 64 (over y, z).
Axes of the slice: x: 4, y: 4, z: 16, core: 2. Of those that a mesh axis runs over, the one named last changes fastest.
Arguments:
- tokens: bfloat16 [65536, 2048], P(('dp', 'expert')), may hold values from -6 to 6
- out_grad: bfloat16 [65536, 2048], P(('dp', 'expert')), may hold values from -6 to 6
- route_gates: float32 [65536, 2], P(('dp', 'expert')), may hold values from 0.1 to 1
- route_slot: int32 [65536, 2], P(('dp', 'expert')), may hold values from 0 to 63, all different within a row; in each aligned block of 128 rows (0 to 127, 128 to 255, ...) at most 5 rows name the same one
- gate_weight: bfloat16 [64, 2048, 768], P('expert', 'dp'), may hold values from -0.125 to 0.125
- up_weight: bfloat16 [64, 2048, 768], P('expert', 'dp'), may hold values from -0.125 to 0.125
- down_weight: bfloat16 [64, 2048, 768], P('expert', 'dp'), may hold values from -0.21875 to 0.21875
Outputs:
- moe_out: bfloat16 [65536, 2048], P(('dp', 'expert'))
- token_grad: bfloat16 [65536, 2048], P(('dp', 'expert'))
- down_grad: bfloat16 [64, 2048, 768], P('expert', 'dp')
Inputs may be any that keep to these rules, and one draw needn't show every extreme that they name: `route_slot`: the 2 routes of a token name different slots. At most 5 routes of the tokens of one device name one slot, and in every draw some device sends exactly 5 routes to some slot.
All inputs are finite; a program needn't handle non-finite values.
Results may differ from a plain program's by a relative error of at most 0.014.
Values may be sent and summed in bfloat16 or wider, within the bound.
A program may use at most 64 MiB of HBM per device.

v0:
```python
import jax
import jax.numpy as jnp
from jax import lax
from jax.sharding import PartitionSpec as P


def expert_forward(rows_in, w_gate, w_up, w_down):
    gate_proj = jnp.dot(rows_in, w_gate, preferred_element_type=jnp.float32)
    up_proj = jnp.dot(rows_in, w_up, preferred_element_type=jnp.float32)
    sigma_gate = jax.nn.sigmoid(gate_proj)
    activated = gate_proj * sigma_gate
    hidden = (activated * up_proj).astype(jnp.bfloat16)
    outputs = lax.dot_general(
        hidden, w_down, (((1,), (1,)), ((), ())), preferred_element_type=jnp.float32
    ).astype(jnp.bfloat16)
    return (outputs, gate_proj, up_proj, hidden)


def expert_backward(rows_grad, gate_proj, up_proj, w_gate, w_up, w_down):
    grad_hidden = jnp.dot(rows_grad, w_down, preferred_element_type=jnp.float32)
    sigma_gate = jax.nn.sigmoid(gate_proj)
    activated = gate_proj * sigma_gate
    grad_gate = (
        grad_hidden * up_proj * sigma_gate * (1.0 + gate_proj * (1.0 - sigma_gate))
    ).astype(jnp.bfloat16)
    grad_up = (grad_hidden * activated).astype(jnp.bfloat16)
    contract_dims = (((1,), (1,)), ((), ()))
    summed = lax.dot_general(
        grad_gate, w_gate, contract_dims, preferred_element_type=jnp.float32
    ) + lax.dot_general(grad_up, w_up, contract_dims, preferred_element_type=jnp.float32)
    return summed.astype(jnp.bfloat16)


def per_device(tokens, out_grad, route_gates, route_slot, gate_weight, up_weight, down_weight):
    tok_dev, model_width = tokens.shape
    route_count = route_slot.shape[1]
    peer_count = lax.axis_size("expert")
    capacity = max(2, (5 * tok_dev * route_count + 4 * peer_count - 1) // (4 * peer_count))
    route_total = tok_dev * route_count
    send_rows = peer_count * capacity
    flat_slot = route_slot.reshape(-1)
    onehot = (flat_slot[:, None] == jnp.arange(peer_count, dtype=jnp.int32)[None, :]).astype(
        jnp.int32
    )
    slot_rank = jnp.sum((jnp.cumsum(onehot, axis=0) - onehot) * onehot, axis=1)
    send_index = flat_slot * capacity + slot_rank
    route_of_row = (
        jnp.full((send_rows,), route_total, jnp.int32)
        .at[send_index]
        .set(jnp.arange(route_total, dtype=jnp.int32))
    )
    filled = route_of_row < route_total
    safe_route = jnp.where(filled, route_of_row, 0)
    token_row = safe_route // route_count
    gate_value = jnp.where(filled, route_gates.reshape(-1)[safe_route], 0.0)
    rows_in = jnp.where(filled[:, None], tokens[token_row], jnp.zeros((), tokens.dtype))
    rows_in = rows_in.reshape(peer_count, capacity, model_width)
    rows_grad = (gate_value[:, None] * out_grad[token_row].astype(jnp.float32)).astype(jnp.bfloat16)
    rows_grad = rows_grad.reshape(peer_count, capacity, model_width)
    full_gate, full_up, full_down = (
        lax.all_gather(gate_weight, "dp", axis=1, tiled=True),
        lax.all_gather(up_weight, "dp", axis=1, tiled=True),
        lax.all_gather(down_weight, "dp", axis=1, tiled=True),
    )
    w_gate = full_gate[0]
    w_up = full_up[0]
    w_down = full_down[0]
    item_shape = (peer_count, capacity, model_width)
    received = lax.all_to_all(rows_in, "expert", split_axis=0, concat_axis=0, tiled=True)
    outputs, gate_proj, up_proj, hidden_saved = expert_forward(
        received.reshape(-1, model_width), w_gate, w_up, w_down
    )
    out_back = lax.all_to_all(
        outputs.reshape(item_shape), "expert", split_axis=0, concat_axis=0, tiled=True
    )
    grad_in = lax.all_to_all(rows_grad, "expert", split_axis=0, concat_axis=0, tiled=True)
    grad_rows = expert_backward(
        grad_in.reshape(-1, model_width), gate_proj, up_proj, w_gate, w_up, w_down
    )
    grad_back = lax.all_to_all(
        grad_rows.reshape(item_shape), "expert", split_axis=0, concat_axis=0, tiled=True
    )
    grad_flat = grad_in.reshape(-1, model_width)
    down_share = lax.psum_scatter(
        lax.dot_general(
            grad_flat, hidden_saved, (((0,), (0,)), ((), ())), preferred_element_type=jnp.float32
        ).astype(jnp.bfloat16),
        "dp",
        scatter_dimension=0,
        tiled=True,
    )
    down_grad = down_share[None]
    out_routes = out_back.reshape(send_rows, model_width)[send_index].astype(jnp.float32)
    out_routes = out_routes.reshape(tok_dev, route_count, model_width)
    moe_out = jnp.sum(route_gates[:, :, None] * out_routes, axis=1).astype(jnp.bfloat16)
    grad_routes = grad_back.reshape(send_rows, model_width)[send_index].astype(jnp.float32)
    token_grad = jnp.sum(grad_routes.reshape(tok_dev, route_count, model_width), axis=1).astype(
        jnp.bfloat16
    )
    return (moe_out, token_grad, down_grad)


def solution(mesh):
    placed = (
        P(("dp", "expert"), None),
        P(("dp", "expert"), None),
        P(("dp", "expert"), None),
        P(("dp", "expert"), None),
        P("expert", "dp", None),
        P("expert", "dp", None),
        P("expert", "dp", None),
    )
    return jax.shard_map(
        per_device,
        mesh=mesh,
        in_specs=placed,
        out_specs=(P(("dp", "expert"), None), P(("dp", "expert"), None), P("expert", "dp", None)),
        check_vma=False,
    )
```

profile of v0, /device:TPU:6, one launch (start us, length us, event | category | flops | bytes accessed | tf_op | source)
XLA Modules:
  0.0 502.2 jit_solution(14308860593216181673)
XLA Ops:
  13.3 2.5 gather_fusion.2
  20.6 3.8 multiply_convert_fusion
  24.4 18.9 %all-to-all-start.2 = ((bf16[64,5,2048]{2,1,0:T(8,128)(2,1)}), bf16[64,5,2048]{2,1,0:T(8,128)(2,1)S(1)}, u32[]{:S(2)}, u32[]{:S(2)}) async-start(bf16[64,5,2048]{2,1,0:T(8,128)(2,1)} %multiply_convert_fusion), calls=%async_computation.2 | async-start | bytes 4194304 | tf_op jit(solution)/shard_map/all_to_all | solution.py:76
  44.1 3.0 gather_fusion
  47.2 3.4 gather.20
  50.5 3.3 broadcast_select_fusion
  53.8 87.0 %all-to-all-done.2 = bf16[64,5,2048]{2,1,0:T(8,128)(2,1)S(1)} async-done(((bf16[64,5,2048]{2,1,0:T(8,128)(2,1)}), bf16[64,5,2048]{2,1,0:T(8,128)(2,1)S(1)}, u32[]{:S(2)}, u32[]{:S(2)}) %all-to-all-start.2) | async-done | bytes 1310752 | tf_op jit(solution)/shard_map/all_to_all | solution.py:76
  140.8 8.2 %all-to-all-start = ((bf16[64,5,2048]{2,1,0:T(8,128)(2,1)}), bf16[64,5,2048]{2,1,0:T(8,128)(2,1)}, u32[]{:S(2)}, u32[]{:S(2)}) async-start(bf16[64,5,2048]{2,1,0:T(8,128)(2,1)} %broadcast_select_fusion), calls=%async_computation | async-start | bytes 4194304 | tf_op jit(solution)/shard_map/all_to_all | solution.py:69
  151.3 95.4 %all-to-all-done = bf16[64,5,2048]{2,1,0:T(8,128)(2,1)} async-done(((bf16[64,5,2048]{2,1,0:T(8,128)(2,1)}), bf16[64,5,2048]{2,1,0:T(8,128)(2,1)}, u32[]{:S(2)}, u32[]{:S(2)}) %all-to-all-start) | async-done | bytes 1310752 | tf_op jit(solution)/shard_map/all_to_all | solution.py:69
  246.6 2.6 reshape.100
  249.2 4.1 fusion
  253.3 4.1 fusion.10
  257.4 4.3 multiply_convert_fusion.3
  267.0 8.1 %all-to-all-start.3 = ((bf16[64,5,2048]{2,1,0:T(8,128)(2,1)}), bf16[64,5,2048]{2,1,0:T(8,128)(2,1)S(1)}, u32[]{:S(2)}, u32[]{:S(2)}) async-start(bf16[64,5,2048]{2,1,0:T(8,128)(2,1)} %reshape.105), calls=%async_computation.3 | async-start | bytes 4194304 | tf_op jit(solution)/shard_map/all_to_all | solution.py:80
  275.2 4.8 convolution_convert_fusion
  280.0 4.2 fusion.18
  284.2 3.4 reshape.101
  287.6 85.2 %all-to-all-done.3 = bf16[64,5,2048]{2,1,0:T(8,128)(2,1)S(1)} async-done(((bf16[64,5,2048]{2,1,0:T(8,128)(2,1)}), bf16[64,5,2048]{2,1,0:T(8,128)(2,1)S(1)}, u32[]{:S(2)}, u32[]{:S(2)}) %all-to-all-start.3) | async-done | bytes 1310752 | tf_op jit(solution)/shard_map/all_to_all | solution.py:80
  374.1 8.5 %all-to-all-start.1 = ((bf16[64,5,2048]{2,1,0:T(8,128)(2,1)}), bf16[64,5,2048]{2,1,0:T(8,128)(2,1)}, u32[]{:S(2)}, u32[]{:S(2)}) async-start(bf16[64,5,2048]{2,1,0:T(8,128)(2,1)} %reshape.101), calls=%async_computation.1 | async-start | bytes 4194304 | tf_op jit(solution)/shard_map/all_to_all | solution.py:73
  382.6 2.6 reshape.106
  388.1 91.8 %all-to-all-done.1 = bf16[64,5,2048]{2,1,0:T(8,128)(2,1)} async-done(((bf16[64,5,2048]{2,1,0:T(8,128)(2,1)}), bf16[64,5,2048]{2,1,0:T(8,128)(2,1)}, u32[]{:S(2)}, u32[]{:S(2)}) %all-to-all-start.1) | async-done | bytes 1310752 | tf_op jit(solution)/shard_map/all_to_all | solution.py:73
  479.9 2.6 reshape.102
  487.2 4.6 reduce_sum.35
  491.7 3.9 multiply_reduce_fusion
  (67 shorter events, 28.0 us)
Async XLA Ops:
  7.2 8.8 %copy-start = (bf16[128,2048]{1,0:T(8,128)(2,1)S(1)}, bf16[128,2048]{1,0:T(8,128)(2,1)}, u32[]{:S(2)}) copy-start(bf16[128,2048]{1,0:T(8,128)(2,1)} %param.8) | copy-start | bytes 1572868
  7.2 242.0 %all-gather.8.cloned.1.call-start = ((), (), s32[]{:S(2)}) async-start(), calls=%async_computation.7 | async-start | bytes 3538944 | tf_op jit(solution)/shard_map/all_gather | solution.py:63
  24.4 19.8 %copy-start.1 = (bf16[128,2048]{1,0:T(8,128)(2,1)S(1)}, bf16[128,2048]{1,0:T(8,128)(2,1)}, u32[]{:S(2)}) copy-start(bf16[128,2048]{1,0:T(8,128)(2,1)} %param.7) | copy-start | bytes 1572868
  24.4 116.5 %all-to-all-start.2 = ((bf16[64,5,2048]{2,1,0:T(8,128)(2,1)}), bf16[64,5,2048]{2,1,0:T(8,128)(2,1)S(1)}, u32[]{:S(2)}, u32[]{:S(2)}) async-start(bf16[64,5,2048]{2,1,0:T(8,128)(2,1)} %multiply_convert_fusion), calls=%async_computation.2 | async-start | bytes 4194304 | tf_op jit(solution)/shard_map/all_to_all | solution.py:76
  43.2 210.1 %all-gather.4.cloned.1.call-start = ((), (), s32[]{:S(2)}) async-start(), calls=%async_computation.5 | async-start | bytes 3538944 | tf_op jit(solution)/shard_map/all_gather | solution.py:61
  140.8 105.8 %all-to-all-start = ((bf16[64,5,2048]{2,1,0:T(8,128)(2,1)}), bf16[64,5,2048]{2,1,0:T(8,128)(2,1)}, u32[]{:S(2)}, u32[]{:S(2)}) async-start(bf16[64,5,2048]{2,1,0:T(8,128)(2,1)} %broadcast_select_fusion), calls=%async_computation | async-start | bytes 4194304 | tf_op jit(solution)/shard_map/all_to_all | solution.py:69
  149.1 108.3 %all-gather.6.cloned.1.call-start = ((), (), s32[]{:S(2)}) async-start(), calls=%async_computation.6 | async-start | bytes 3538944 | tf_op jit(solution)/shard_map/all_gather | solution.py:62
  151.2 98.0 %copy-start.3 = (bf16[320,2048]{1,0:T(8,128)(2,1)S(1)}, bf16[320,2048]{1,0:T(8,128)(2,1)}, u32[]{:S(2)}) copy-start(bf16[320,2048]{1,0:T(8,128)(2,1)} %reshape.104) | copy-start | bytes 3932164
  257.4 4.3 copy-start.6
  257.4 4.3 copy-start.5
  257.4 4.3 copy-start.8
  261.7 1.9 copy-start.4
  261.7 2.1 copy-start.7
  266.9 8.2 %copy-start.9 = (bf16[320,768]{1,0:T(8,128)(2,1)S(1)}, bf16[320,768]{1,0:T(8,128)(2,1)}, u32[]{:S(2)}) copy-start(bf16[320,768]{1,0:T(8,128)(2,1)} %get-tuple-element.5) | copy-start | bytes 1474564
  267.0 105.8 %all-to-all-start.3 = ((bf16[64,5,2048]{2,1,0:T(8,128)(2,1)}), bf16[64,5,2048]{2,1,0:T(8,128)(2,1)S(1)}, u32[]{:S(2)}, u32[]{:S(2)}) async-start(bf16[64,5,2048]{2,1,0:T(8,128)(2,1)} %reshape.105), calls=%async_computation.3 | async-start | bytes 4194304 | tf_op jit(solution)/shard_map/all_to_all | solution.py:80
  275.1 220.6 %reduce-scatter.2.cloned.1.call-start = ((), (), s32[]{:S(2)}) async-start(), calls=%async_computation.8 | async-start | bytes 3538944 | tf_op jit(solution)/shard_map/reduce_scatter | solution.py:84
  372.8 1.4 copy-start.2
  374.1 105.8 %all-to-all-start.1 = ((bf16[64,5,2048]{2,1,0:T(8,128)(2,1)}), bf16[64,5,2048]{2,1,0:T(8,128)(2,1)}, u32[]{:S(2)}, u32[]{:S(2)}) async-start(bf16[64,5,2048]{2,1,0:T(8,128)(2,1)} %reshape.101), calls=%async_computation.1 | async-start | bytes 4194304 | tf_op jit(solution)/shard_map/all_to_all | solution.py:73
Sparse Core Ops, SparseCore 0:
  10.1 38.7 all-gather.7
  51.0 35.3 all-gather.3
  152.0 35.0 all-gather.5
  280.1 41.6 reduce-scatter.1
where the time goes:
time: 504 us; the launch traced here: 502 us
  waiting for transfers between devices  361 us (72%)
  starting transfers between devices  44.1 us (9%)
  local copies, waits for them, and re-layouts  41.6 us (8%)
  matrix products  24.1 us (5%)
  other arithmetic  17.1 us (3%)
  between operations  14 us (3%)
    all_to_all x1, waiting for transfers between devices, per_device(): lax.all_to_all(rows_in, 'expert', split_axis=0, concat_axis=0, tiled=True)  95.4 us
    all_to_all x1, waiting for transfers between devices, per_device(): lax.all_to_all(outputs.reshape(item_shape), 'expert', split_axis=0, conca...  91.8 us
    all_to_all x1, waiting for transfers between devices, per_device(): lax.all_to_all(rows_grad, 'expert', split_axis=0, concat_axis=0, tiled=True)  87 us
    all_to_all x1, waiting for transfers between devices, per_device(): lax.all_to_all(grad_rows.reshape(item_shape), 'expert', split_axis=0, con...  85.2 us
    all_to_all x1, starting transfers between devices, per_device(): lax.all_to_all(rows_grad, 'expert', split_axis=0, concat_axis=0, tiled=True)  18.9 us
  transfers between devices with their start and end apart: 8, of which 4 were waited for; matrix products, arithmetic and copies ran while one was open for 14% of the time, Pallas kernels for 0%

commit v1 on v0

--- a/solution.py
+++ b/solution.py
@@ -2,6 +2,8 @@
 import jax.numpy as jnp
 from jax import lax
 from jax.sharding import PartitionSpec as P
+
+LANES = 128
 
 
 def expert_forward(rows_in, w_gate, w_up, w_down):
@@ -53,10 +55,15 @@
     safe_route = jnp.where(filled, route_of_row, 0)
     token_row = safe_route // route_count
     gate_value = jnp.where(filled, route_gates.reshape(-1)[safe_route], 0.0)
-    rows_in = jnp.where(filled[:, None], tokens[token_row], jnp.zeros((), tokens.dtype))
-    rows_in = rows_in.reshape(peer_count, capacity, model_width)
-    rows_grad = (gate_value[:, None] * out_grad[token_row].astype(jnp.float32)).astype(jnp.bfloat16)
-    rows_grad = rows_grad.reshape(peer_count, capacity, model_width)
+    tile = (model_width // LANES, LANES)
+    token_tiles = tokens.reshape(tok_dev, *tile)
+    grad_tiles = out_grad.reshape(tok_dev, *tile)
+    rows_in = jnp.where(filled[:, None, None], token_tiles[token_row], jnp.zeros((), tokens.dtype))
+    rows_in = rows_in.reshape(peer_count, capacity * tile[0], LANES)
+    rows_grad = (
+        gate_value[:, None, None] * grad_tiles[token_row].astype(jnp.float32)
+    ).astype(jnp.bfloat16)
+    rows_grad = rows_grad.reshape(peer_count, capacity * tile[0], LANES)
     full_gate, full_up, full_down = (
         lax.all_gather(gate_weight, "dp", axis=1, tiled=True),
         lax.all_gather(up_weight, "dp", axis=1, tiled=True),
@@ -65,7 +72,7 @@
     w_gate = full_gate[0]
     w_up = full_up[0]
     w_down = full_down[0]
-    item_shape = (peer_count, capacity, model_width)
+    item_shape = (peer_count, capacity * tile[0], LANES)
     received = lax.all_to_all(rows_in, "expert", split_axis=0, concat_axis=0, tiled=True)
     outputs, gate_proj, up_proj, hidden_saved = expert_forward(
         received.reshape(-1, model_width), w_gate, w_up, w_down
@@ -90,13 +97,15 @@
         tiled=True,
     )
     down_grad = down_share[None]
-    out_routes = out_back.reshape(send_rows, model_width)[send_index].astype(jnp.float32)
-    out_routes = out_routes.reshape(tok_dev, route_count, model_width)
-    moe_out = jnp.sum(route_gates[:, :, None] * out_routes, axis=1).astype(jnp.bfloat16)
-    grad_routes = grad_back.reshape(send_rows, model_width)[send_index].astype(jnp.float32)
-    token_grad = jnp.sum(grad_routes.reshape(tok_dev, route_count, model_width), axis=1).astype(
+    out_routes = out_back.reshape(send_rows, *tile)[send_index].astype(jnp.float32)
+    out_routes = out_routes.reshape(tok_dev, route_count, *tile)
+    moe_out = jnp.sum(route_gates[:, :, None, None] * out_routes, axis=1).astype(jnp.bfloat16)
+    moe_out = moe_out.reshape(tok_dev, model_width)
+    grad_routes = grad_back.reshape(send_rows, *tile)[send_index].astype(jnp.float32)
+    token_grad = jnp.sum(grad_routes.reshape(tok_dev, route_count, *tile), axis=1).astype(
         jnp.bfloat16
     )
+    token_grad = token_grad.reshape(tok_dev, model_width)
     return (moe_out, token_grad, down_grad)
 
 

time: 504 us -> 328 us (0.65)
  waiting for transfers between devices: 361 us -> 223 us
  local copies, waits for them, and re-layouts: 41.6 us -> 23 us
  other arithmetic: 17.1 us -> 6.02 us
    all_to_all x1, waiting for transfers between devices: 91.8 us -> 49.2 us  [per_device(): lax.all_to_all(outputs.reshape(item_shape), 'expert', split_axis=0, conca...]
    all_to_all x1, waiting for transfers between devices: 87 us -> 45.2 us  [per_device(): lax.all_to_all(rows_grad, 'expert', split_axis=0, concat_axis=0, tiled=True)]
    all_to_all x1, waiting for transfers between devices: 95.4 us -> 57.6 us  [per_device(): lax.all_to_all(rows_in, 'expert', split_axis=0, concat_axis=0, tiled=True)]
    all_to_all x1, waiting for transfers between devices: 85.2 us -> 63.5 us  [per_device(): lax.all_to_all(grad_rows.reshape(item_shape), 'expert', split_axis=0, con...]
    all_to_all x1, starting transfers between devices: 18.9 us -> 6.7 us  [per_device(): lax.all_to_all(rows_grad, 'expert', split_axis=0, concat_axis=0, tiled=True)]
    all_to_all x1, starting transfers between devices: 8.25 us -> 18.9 us  [per_device(): lax.all_to_all(rows_in, 'expert', split_axis=0, concat_axis=0, tiled=True)]
    reduce_sum x2, other arithmetic: 8.49 us -> 0.6 us  [the longest x1 0.36 us: per_device(): jnp.sum(route_gates[:, :, None, None] * out_routes, axis=1)]
    gather x6 -> x4, local copies, waits for them, and re-layouts: 14 us -> 6.33 us  [the longest x1 1.86 us: per_device(): grad_tiles[token_row].astype(jnp.float32)]
  transfers between devices with their start and end apart: 8 -> 8, of which waited for: 4 -> 5; matrix products, arithmetic and copies ran while one was open for 14% -> 15% of each run, Pallas kernels for 0% -> 0%
where the time goes in v1:
time: 328 us
  waiting for transfers between devices  223 us (68%)
  starting transfers between devices  39.3 us (12%)
  local copies, waits for them, and re-layouts  23 us (7%)
  matrix products  22.6 us (7%)
  between operations  14.1 us (4%)
  other arithmetic  6.02 us (2%)
    all_to_all x1, waiting for transfers between devices, per_device(): lax.all_to_all(grad_rows.reshape(item_shape), 'expert', split_axis=0, con...  63.5 us
    all_to_all x1, waiting for transfers between devices, per_device(): lax.all_to_all(rows_in, 'expert', split_axis=0, concat_axis=0, tiled=True)  57.6 us
    all_to_all x1, waiting for transfers between devices, per_device(): lax.all_to_all(outputs.reshape(item_shape), 'expert', split_axis=0, conca...  49.2 us
    all_to_all x1, waiting for transfers between devices, per_device(): lax.all_to_all(rows_grad, 'expert', split_axis=0, concat_axis=0, tiled=True)  45.2 us
    all_to_all x1, starting transfers between devices, per_device(): lax.all_to_all(rows_in, 'expert', split_axis=0, concat_axis=0, tiled=True)  18.9 us
    all_to_all x1, starting transfers between devices, per_device(): lax.all_to_all(outputs.reshape(item_shape), 'expert', split_axis=0, conca...  6.72 us
    all_to_all x1, starting transfers between devices, per_device(): lax.all_to_all(grad_rows.reshape(item_shape), 'expert', split_axis=0, con...  6.72 us
    all_to_all x1, starting transfers between devices, per_device(): lax.all_to_all(rows_grad, 'expert', split_axis=0, concat_axis=0, tiled=True)  6.7 us
  transfers between devices with their start and end apart: 8, of which 5 were waited for; matrix products, arithmetic and copies ran while one was open for 15% of the time, Pallas kernels for 0%

profile of v1, /device:TPU:6, one launch (start us, length us, event | category | flops | bytes accessed | tf_op | source)
XLA Modules:
  0.0 327.8 jit_solution(3888365520433656058)
XLA Ops:
  13.6 1.9 gather_fusion
  15.5 2.2 bitcast_select_fusion
  17.7 18.9 %all-to-all-start = ((bf16[64,80,128]{2,1,0:T(8,128)(2,1)}), bf16[64,80,128]{2,1,0:T(8,128)(2,1)S(1)}, u32[]{:S(2)}, u32[]{:S(2)}) async-start(bf16[64,80,128]{2,1,0:T(8,128)(2,1)} %bitcast_select_fusion), calls=%async_computation | async-start | bytes 2621440 | tf_op jit(solution)/shard_map/all_to_all | solution.py:76
  37.6 2.5 gather_fusion.2
  40.5 1.9 gather_fusion.3
  42.4 1.7 fusion.21
  44.1 57.6 %all-to-all-done = bf16[64,80,128]{2,1,0:T(8,128)(2,1)S(1)} async-done(((bf16[64,80,128]{2,1,0:T(8,128)(2,1)}), bf16[64,80,128]{2,1,0:T(8,128)(2,1)S(1)}, u32[]{:S(2)}, u32[]{:S(2)}) %all-to-all-start) | async-done | bytes 1310752 | tf_op jit(solution)/shard_map/all_to_all | solution.py:76
  101.7 6.7 %all-to-all-start.2 = ((bf16[64,80,128]{2,1,0:T(8,128)(2,1)}), bf16[64,80,128]{2,1,0:T(8,128)(2,1)S(1)}, u32[]{:S(2)}, u32[]{:S(2)}) async-start(bf16[64,80,128]{2,1,0:T(8,128)(2,1)} %fusion.21), calls=%async_computation.2 | async-start | bytes 2621440 | tf_op jit(solution)/shard_map/all_to_all | solution.py:83
  108.4 1.4 reshape.113
  109.9 4.6 %fusion.10 = f32[320,768]{1,0:T(8,128)} fusion(bf16[320,2048]{1,0:T(8,128)(2,1)} %reshape.113, bf16[1,2048,768]{2,1,0:T(8,128)(2,1)} %all-gather.4.cloned.1.call-done), kind=kOutput, calls=%fused_computation.17 | convolution fusion | flops 1006632960 | bytes 5439488 | tf_op jit(solution)/shard_map/dot_general | solution.py:10
  114.4 4.3 %multiply_convert_fusion.2 = (bf16[320,768]{1,0:T(8,128)(2,1)S(1)}, f32[320,768]{1,0:T(8,128)}) fusion(f32[320,768]{1,0:T(8,128)} %fusion.10, bf16[320,2048]{1,0:T(8,128)(2,1)S(1)} %copy-done.2, bf16[1,2048,768]{2,1,0:T(8,128)(2,1)} %all-gather.6.cloned.1.call-done), kind=kOutput, calls=%fused_computation.30 | convolution fusion | flops 1008107520 | bytes 6914048 | tf_op jit(solution)/shard_map/dot_general | solution.py:11
  118.7 5.2 %all-gather.8.cloned.1.call-done = bf16[1,2048,768]{2,1,0:T(8,128)(2,1)} async-done(((bf16[1,256,768]{2,1,0:T(8,128)(2,1)}), bf16[1,2048,768]{2,1,0:T(8,128)(2,1)}) %all-gather.8.cloned.1.call-update) | async-done | bytes 3145744 | tf_op jit(solution)/shard_map/all_gather | solution.py:70
  123.9 3.1 fusion.18
  127.0 1.5 reshape.114
  128.5 45.2 %all-to-all-done.2 = bf16[64,80,128]{2,1,0:T(8,128)(2,1)S(1)} async-done(((bf16[64,80,128]{2,1,0:T(8,128)(2,1)}), bf16[64,80,128]{2,1,0:T(8,128)(2,1)S(1)}, u32[]{:S(2)}, u32[]{:S(2)}) %all-to-all-start.2) | async-done | bytes 1310752 | tf_op jit(solution)/shard_map/all_to_all | solution.py:83
  173.7 6.7 %all-to-all-start.1 = ((bf16[64,80,128]{2,1,0:T(8,128)(2,1)}), bf16[64,80,128]{2,1,0:T(8,128)(2,1)S(1)}, u32[]{:S(2)}, u32[]{:S(2)}) async-start(bf16[64,80,128]{2,1,0:T(8,128)(2,1)} %reshape.114), calls=%async_computation.1 | async-start | bytes 2621440 | tf_op jit(solution)/shard_map/all_to_all | solution.py:80
  180.6 1.4 reshape.118
  182.1 4.8 %convolution_convert_fusion = bf16[2048,768]{1,0:T(8,128)(2,1)} fusion(bf16[320,2048]{1,0:T(8,128)(2,1)} %reshape.118, bf16[320,768]{1,0:T(8,128)(2,1)S(1)} %get-tuple-element.5), kind=kOutput, calls=%fused_computation.6 | convolution fusion | flops 1008205824 | bytes 4947968 | tf_op jit(solution)/shard_map/dot_general | solution.py:92
  188.2 3.2 fusion
  194.9 1.5 reshape.119
  196.4 49.2 %all-to-all-done.1 = bf16[64,80,128]{2,1,0:T(8,128)(2,1)S(1)} async-done(((bf16[64,80,128]{2,1,0:T(8,128)(2,1)}), bf16[64,80,128]{2,1,0:T(8,128)(2,1)S(1)}, u32[]{:S(2)}, u32[]{:S(2)}) %all-to-all-start.1) | async-done | bytes 1310752 | tf_op jit(solution)/shard_map/all_to_all | solution.py:80
  245.6 6.7 %all-to-all-start.3 = ((bf16[64,80,128]{2,1,0:T(8,128)(2,1)}), bf16[64,80,128]{2,1,0:T(8,128)(2,1)S(1)}, u32[]{:S(2)}, u32[]{:S(2)}) async-start(bf16[64,80,128]{2,1,0:T(8,128)(2,1)} %reshape.119), calls=%async_computation.3 | async-start | bytes 2621440 | tf_op jit(solution)/shard_map/all_to_all | solution.py:87
  252.4 1.8 gather_fusion.1
  254.1 63.5 %all-to-all-done.3 = bf16[64,80,128]{2,1,0:T(8,128)(2,1)S(1)} async-done(((bf16[64,80,128]{2,1,0:T(8,128)(2,1)}), bf16[64,80,128]{2,1,0:T(8,128)(2,1)S(1)}, u32[]{:S(2)}, u32[]{:S(2)}) %all-to-all-start.3) | async-done | bytes 1310752 | tf_op jit(solution)/shard_map/all_to_all | solution.py:87
  (70 shorter events, 16.4 us)
Async XLA Ops:
  7.2 6.3 %copy-start.3 = (bf16[128,2048]{1,0:T(8,128)(2,1)S(1)}, bf16[128,2048]{1,0:T(8,128)(2,1)}, u32[]{:S(2)}) copy-start(bf16[128,2048]{1,0:T(8,128)(2,1)} %param.7) | copy-start | bytes 1572868
  7.2 102.7 %all-gather.4.cloned.1.call-start = ((), (), s32[]{:S(2)}) async-start(), calls=%async_computation.5 | async-start | bytes 3538944 | tf_op jit(solution)/shard_map/all_gather | solution.py:68
  7.9 106.5 %all-gather.6.cloned.1.call-start = ((), (), s32[]{:S(2)}) async-start(), calls=%async_computation.6 | async-start | bytes 3538944 | tf_op jit(solution)/shard_map/all_gather | solution.py:69
  17.7 19.6 %copy-start.5 = (f32[128,2]{0,1:T(2,128)S(1)}, f32[128,2]{0,1:T(2,128)}, u32[]{:S(2)}) copy-start(f32[128,2]{0,1:T(2,128)} %param.9) | copy-start | bytes 3076
  17.7 84.0 %all-to-all-start = ((bf16[64,80,128]{2,1,0:T(8,128)(2,1)}), bf16[64,80,128]{2,1,0:T(8,128)(2,1)S(1)}, u32[]{:S(2)}, u32[]{:S(2)}) async-start(bf16[64,80,128]{2,1,0:T(8,128)(2,1)} %bitcast_select_fusion), calls=%async_computation | async-start | bytes 2621440 | tf_op jit(solution)/shard_map/all_to_all | solution.py:76
  36.6 87.3 %all-gather.8.cloned.1.call-start = ((), (), s32[]{:S(2)}) async-start(), calls=%async_computation.7 | async-start | bytes 3538944 | tf_op jit(solution)/shard_map/all_gather | solution.py:70
  37.3 3.1 copy-start.4
  101.7 71.9 %all-to-all-start.2 = ((bf16[64,80,128]{2,1,0:T(8,128)(2,1)}), bf16[64,80,128]{2,1,0:T(8,128)(2,1)S(1)}, u32[]{:S(2)}, u32[]{:S(2)}) async-start(bf16[64,80,128]{2,1,0:T(8,128)(2,1)} %fusion.21), calls=%async_computation.2 | async-start | bytes 2621440 | tf_op jit(solution)/shard_map/all_to_all | solution.py:83
  109.8 4.6 %copy-start.2 = (bf16[320,2048]{1,0:T(8,128)(2,1)S(1)}, bf16[320,2048]{1,0:T(8,128)(2,1)}, u32[]{:S(2)}) copy-start(bf16[320,2048]{1,0:T(8,128)(2,1)} %reshape.113) | copy-start | bytes 3932164
  173.7 72.0 %all-to-all-start.1 = ((bf16[64,80,128]{2,1,0:T(8,128)(2,1)}), bf16[64,80,128]{2,1,0:T(8,128)(2,1)S(1)}, u32[]{:S(2)}, u32[]{:S(2)}) async-start(bf16[64,80,128]{2,1,0:T(8,128)(2,1)} %reshape.114), calls=%async_computation.1 | async-start | bytes 2621440 | tf_op jit(solution)/shard_map/all_to_all | solution.py:80
  180.4 140.9 %reduce-scatter.2.cloned.1.call-start = ((), (), s32[]{:S(2)}) async-start(), calls=%async_computation.8 | async-start | bytes 3538944 | tf_op jit(solution)/shard_map/reduce_scatter | solution.py:91
  186.9 1.3 copy-start.1
  188.2 3.2 copy-start.7
  188.2 3.2 copy-start.8
  191.4 1.9 copy-start.6
  191.4 2.1 copy-start.9
  245.6 72.0 %all-to-all-start.3 = ((bf16[64,80,128]{2,1,0:T(8,128)(2,1)}), bf16[64,80,128]{2,1,0:T(8,128)(2,1)S(1)}, u32[]{:S(2)}, u32[]{:S(2)}) async-start(bf16[64,80,128]{2,1,0:T(8,128)(2,1)} %reshape.119), calls=%async_computation.3 | async-start | bytes 2621440 | tf_op jit(solution)/shard_map/all_to_all | solution.py:87
  318.5 1.2 copy-start
Sparse Core Ops, SparseCore 0:
  10.1 38.7 all-gather.3
  51.0 35.3 all-gather.5
  88.5 35.3 all-gather.7
  187.0 41.5 reduce-scatter.1

commit v2 on v0

v2 whole, which is shorter than its diff:
```python
import functools

import jax
import jax.numpy as jnp
from jax import lax
from jax.experimental import pallas as pl
from jax.experimental.pallas import tpu as pltpu
from jax.sharding import PartitionSpec as P

LANES = 128
SUB = 16
NX, NY, NZ = 4, 4, 16
BACK = NZ - 1
WIDE = 256
MESH = pl.DeviceIdType.MESH
X, DY, Y, DX = range(4)


def layer(
    cap,
    row_of_ref,
    gate_of_ref,
    row_of_col_ref,
    gate_of_col_ref,
    tokens_ref,
    grads_ref,
    gate_in,
    up_in,
    down_in,
    moe_ref,
    tgrad_ref,
    dgrad_ref,
    perm,
    w_gate,
    w_up,
    w_down,
    sent,
    got,
    relay,
    rows_x,
    rows_dy,
    rows_tmp,
    slope,
    act,
    hidden,
    d_gate,
    d_up,
    part,
    parts,
    send_sem,
    recv_sem,
    relay_sem,
    pass_sem,
    own_sem,
    w_own,
    w_send,
    w_pass,
    w_recv,
    p_send,
    p_recv,
):
    f32, bf16 = jnp.float32, jnp.bfloat16
    dp, e = lax.axis_index("dp"), lax.axis_index("expert")
    y, z = e // NZ, e % NZ
    chip, core = dp // 2, dp % 2
    n_exp, n_dp = NY * NZ, NX * 2
    rows = n_exp * cap
    width = tokens_ref.shape[1]
    shard = width // n_dp
    ff = hidden.shape[1]
    unit = cap * SUB

    barrier = pltpu.get_barrier_semaphore()

    def greet(k, _):
        pl.semaphore_signal(
            barrier, inc=1, device_id=(dp, (e + k) % n_exp), device_id_type=MESH
        )
        return 0

    lax.fori_loop(1, n_exp, greet, 0)
    for k in range(1, n_dp):
        pl.semaphore_signal(barrier, inc=1, device_id=((dp + k) % n_dp, e), device_id_type=MESH)

    def block(p):
        return pl.ds(pl.multiple_of(p * unit, SUB), unit)

    def owner_rows(p):
        return pl.ds(pl.multiple_of(p * shard, shard), shard)

    def cols(n):
        return pl.ds(pl.multiple_of(n * WIDE, WIDE), WIDE)

    at = lax.broadcasted_iota(jnp.int32, (WIDE, WIDE), 0)
    to = lax.broadcasted_iota(jnp.int32, (WIDE, WIDE), 1)
    perm[...] = jnp.where((at % SUB) * SUB + at // SUB == to, 1.0, 0.0).astype(bf16)

    def to_tiles(nat, flat):
        def step(g, _):
            halves = []
            for h in range(2):
                r = pl.ds(pl.multiple_of(g * 32 + h * SUB, SUB), SUB)
                halves.append(
                    jnp.concatenate(
                        [nat[r, j * LANES : (j + 1) * LANES] for j in range(SUB)], axis=0
                    )
                )
            moved = jnp.dot(
                perm[...], jnp.concatenate(halves, axis=1), preferred_element_type=f32
            ).astype(bf16)
            for h in range(2):
                r = pl.ds(pl.multiple_of(g * 512 + h * WIDE, WIDE), WIDE)
                flat[r, :] = moved[:, h * LANES : (h + 1) * LANES]
            return 0

        lax.fori_loop(0, rows // 32, step, 0)

    def to_rows(flat, nat):
        def step(g, _):
            halves = [
                flat[pl.ds(pl.multiple_of(g * 512 + h * WIDE, WIDE), WIDE), :] for h in range(2)
            ]
            moved = jnp.dot(
                perm[...], jnp.concatenate(halves, axis=1), preferred_element_type=f32
            ).astype(bf16)
            for h in range(2):
                r = pl.ds(pl.multiple_of(g * 32 + h * SUB, SUB), SUB)
                for j in range(SUB):
                    nat[r, j * LANES : (j + 1) * LANES] = moved[
                        j * SUB : (j + 1) * SUB, h * LANES : (h + 1) * LANES
                    ]
            return 0

        lax.fori_loop(0, rows // 32, step, 0)

    def send(ph, p):
        pltpu.make_async_remote_copy(
            sent.at[ph, block(p)],
            got.at[ph, block(e)],
            send_sem.at[ph],
            recv_sem.at[ph],
            device_id=(dp, p),
            device_id_type=MESH,
        ).start()

    def exchange(ph):
        far = (z + NZ // 2) % NZ
        for a in (2, 3):
            pltpu.make_async_remote_copy(
                sent.at[ph, block((y + a) % NY * NZ + far)],
                relay.at[ph, pl.ds((a - 2) * unit, unit)],
                send_sem.at[ph],
                relay_sem.at[ph],
                device_id=(dp, y * NZ + (z + BACK) % NZ),
                device_id_type=MESH,
            ).start()
        pltpu.make_async_copy(
            sent.at[ph, block(e)], got.at[ph, block(e)], own_sem.at[ph]
        ).start()
        for a in (0, 1):
            send(ph, (y + a) % NY * NZ + far)

        def step(i, _):
            for a in range(NY):
                send(ph, (y + a) % NY * NZ + (z + i) % NZ)
                send(ph, (y + a) % NY * NZ + (z + NZ // 2 + i) % NZ)
            return 0

        lax.fori_loop(1, NZ // 2, step, 0)
        for a in range(1, NY):
            send(ph, (y + a) % NY * NZ + z)

    def pass_on(ph):
        came = (z + NZ - BACK) % NZ
        pltpu.make_async_remote_copy(
            relay.at[ph],
            relay.at[ph],
            pass_sem.at[ph],
            relay_sem.at[ph],
            device_id=(dp, y * NZ + came),
            device_id_type=MESH,
        ).wait_recv()
        for a in (2, 3):
            pltpu.make_async_remote_copy(
                relay.at[ph, pl.ds((a - 2) * unit, unit)],
                got.at[ph, block(y * NZ + came)],
                pass_sem.at[ph],
                recv_sem.at[ph],
                device_id=(dp, (y + a) % NY * NZ + (came + NZ // 2) % NZ),
                device_id_type=MESH,
            ).start()

    next_e = y * NZ + (z + 1) % NZ

    def arrived(ph):
        most = pl.ds(0, (n_exp - 1) * unit)
        pltpu.make_async_remote_copy(
            sent.at[ph, most],
            got.at[ph, most],
            send_sem.at[ph],
            recv_sem.at[ph],
            device_id=(dp, next_e),
            device_id_type=MESH,
        ).wait_recv()
        pltpu.make_async_copy(
            sent.at[ph, block(e)], got.at[ph, block(e)], own_sem.at[ph]
        ).wait()

    def drained(ph):
        most = pl.ds(0, (n_exp - 1) * unit)
        pltpu.make_async_remote_copy(
            sent.at[ph, most],
            got.at[ph, most],
            send_sem.at[ph],
            recv_sem.at[ph],
            device_id=(dp, next_e),
            device_id_type=MESH,
        ).wait_send()
        pltpu.make_async_remote_copy(
            relay.at[ph],
            relay.at[ph],
            pass_sem.at[ph],
            relay_sem.at[ph],
            device_id=(dp, next_e),
            device_id_type=MESH,
        ).wait_send()

    slot_row = lax.broadcasted_iota(jnp.int32, (rows, tokens_ref.shape[0]), 0)
    hit0 = slot_row == row_of_ref[0:1, :]
    hit1 = slot_row == row_of_ref[1:2, :]
    pick = jnp.where(hit0 | hit1, 1.0, 0.0).astype(bf16)

    def gather_x(n, _):
        rows_tmp[:, cols(n)] = jnp.dot(
            pick, tokens_ref[:, cols(n)], preferred_element_type=f32
        ).astype(bf16)
        return 0

    lax.fori_loop(0, width // WIDE, gather_x, 0)
    to_tiles(rows_tmp, sent.at[X])

    pl.semaphore_wait(barrier, n_exp - 1 + n_dp - 1)

    turn = 1 - 2 * core
    partner = chip * 2 + 1 - core
    ahead = (chip + NX + turn) % NX * 2 + core
    behind = (chip + NX - turn) % NX * 2 + core
    across = (chip + 2) % NX * 2 + core
    stages = ((0, gate_in, w_gate), (1, up_in, w_up), (2, down_in, w_down))
    for kind, src, full in stages:
        pltpu.make_async_copy(src, full.at[owner_rows(dp)], w_own.at[kind]).start()
        for peer in (ahead, behind, partner):
            pltpu.make_async_remote_copy(
                src,
                full.at[owner_rows(dp)],
                w_send.at[kind],
                w_recv.at[kind, dp],
                device_id=(peer, e),
                device_id_type=MESH,
            ).start()

    exchange(X)
    pass_on(X)

    def weight_in(kind, full, owner):
        pltpu.make_async_remote_copy(
            full.at[owner_rows(owner)],
            full.at[owner_rows(owner)],
            w_pass.at[kind],
            w_recv.at[kind, owner],
            device_id=(partner, e),
            device_id_type=MESH,
        ).wait_recv()

    def weight_on(kind, full, owner, peer):
        pltpu.make_async_remote_copy(
            full.at[owner_rows(owner)],
            full.at[owner_rows(owner)],
            w_pass.at[kind],
            w_recv.at[kind, owner],
            device_id=(peer, e),
            device_id_type=MESH,
        ).start()

    for kind, _, full in stages:
        weight_in(kind, full, behind)
        weight_on(kind, full, behind, ahead)
        weight_on(kind, full, behind, partner)
        weight_in(kind, full, ahead)
        weight_on(kind, full, ahead, partner)

    share = jnp.sum(
        jnp.where(hit0, gate_of_ref[0:1, :], 0.0) + jnp.where(hit1, gate_of_ref[1:2, :], 0.0),
        axis=1,
        keepdims=True,
    )

    def gather_dy(n, _):
        taken = jnp.dot(pick, grads_ref[:, cols(n)], preferred_element_type=f32)
        rows_tmp[:, cols(n)] = (share * taken).astype(bf16)
        return 0

    lax.fori_loop(0, width // WIDE, gather_dy, 0)
    to_tiles(rows_tmp, sent.at[DY])
    exchange(DY)

    for kind, _, full in stages:
        weight_in(kind, full, across)
        weight_on(kind, full, across, partner)
    for kind, src, full in stages:
        pltpu.make_async_copy(src, full.at[owner_rows(dp)], w_own.at[kind]).wait()
        for k in range(NX):
            weight_in(kind, full, (chip + k) % NX * 2 + 1 - core)

    arrived(X)
    to_rows(got.at[X], rows_x)

    def forward(n, _):
        gate = jnp.dot(rows_x[...], w_gate[:, cols(n)], preferred_element_type=f32)
        up = jnp.dot(rows_x[...], w_up[:, cols(n)], preferred_element_type=f32)
        sigma = jax.nn.sigmoid(gate)
        activated = gate * sigma
        act[:, cols(n)] = activated
        slope[:, cols(n)] = up * sigma * (1.0 + gate * (1.0 - sigma))
        hidden[:, cols(n)] = (activated * up).astype(bf16)
        return 0

    lax.fori_loop(0, ff // WIDE, forward, 0)
    across_ff = (((1,), (1,)), ((), ()))

    def project(n, _):
        rows_tmp[:, cols(n)] = lax.dot_general(
            hidden[...], w_down[cols(n), :], across_ff, preferred_element_type=f32
        ).astype(bf16)
        return 0

    lax.fori_loop(0, width // WIDE, project, 0)
    to_tiles(rows_tmp, sent.at[Y])
    pass_on(DY)
    exchange(Y)

    arrived(DY)
    to_rows(got.at[DY], rows_dy)

    def backward(n, _):
        d_hidden = jnp.dot(rows_dy[...], w_down[:, cols(n)], preferred_element_type=f32)
        d_gate[:, cols(n)] = (d_hidden * slope[:, cols(n)]).astype(bf16)
        d_up[:, cols(n)] = (d_hidden * act[:, cols(n)]).astype(bf16)
        return 0

    lax.fori_loop(0, ff // WIDE, backward, 0)

    def project_back(n, _):
        rows_tmp[:, cols(n)] = (
            lax.dot_general(d_gate[...], w_gate[cols(n), :], across_ff, preferred_element_type=f32)
            + lax.dot_general(d_up[...], w_up[cols(n), :], across_ff, preferred_element_type=f32)
        ).astype(bf16)
        return 0

    lax.fori_loop(0, width // WIDE, project_back, 0)
    to_tiles(rows_tmp, sent.at[DX])
    pass_on(Y)
    exchange(DX)

    def outer(n, _):
        part[cols(n), :] = lax.dot_general(
            rows_dy[:, cols(n)], hidden[...], (((0,), (0,)), ((), ())), preferred_element_type=f32
        ).astype(bf16)
        return 0

    lax.fori_loop(0, width // WIDE, outer, 0)
    pltpu.make_async_copy(part.at[owner_rows(dp)], parts.at[owner_rows(dp)], own_sem.at[4]).start()
    for k in range(1, n_dp):
        peer = (dp + k) % n_dp
        pltpu.make_async_remote_copy(
            part.at[owner_rows(peer)],
            parts.at[owner_rows(dp)],
            p_send,
            p_recv,
            device_id=(peer, e),
            device_id_type=MESH,
        ).start()

    token_col = lax.broadcasted_iota(jnp.int32, (tokens_ref.shape[0], rows), 1)
    home0 = jnp.where(token_col == row_of_col_ref[:, 0:1], 1.0, 0.0).astype(bf16)
    home1 = jnp.where(token_col == row_of_col_ref[:, 1:2], 1.0, 0.0).astype(bf16)

    arrived(Y)
    to_rows(got.at[Y], rows_tmp)

    def combine(n, _):
        first = jnp.dot(home0, rows_tmp[:, cols(n)], preferred_element_type=f32)
        second = jnp.dot(home1, rows_tmp[:, cols(n)], preferred_element_type=f32)
        moe_ref[:, cols(n)] = (
            gate_of_col_ref[:, 0:1] * first + gate_of_col_ref[:, 1:2] * second
        ).astype(bf16)
        return 0

    lax.fori_loop(0, width // WIDE, combine, 0)
    pass_on(DX)

    others = pl.ds(0, (n_dp - 1) * shard)
    pltpu.make_async_remote_copy(
        part.at[others], parts.at[others], p_send, p_recv, device_id=(partner, e), device_id_type=MESH
    ).wait_recv()
    pltpu.make_async_copy(part.at[owner_rows(dp)], parts.at[owner_rows(dp)], own_sem.at[4]).wait()

    def total(n, _):
        acc = None
        for p in range(n_dp):
            r = pl.ds(pl.multiple_of(p * shard + n * 32, 32), 32)
            term = parts[r, :].astype(f32)
            acc = term if acc is None else acc + term
        dgrad_ref[pl.ds(pl.multiple_of(n * 32, 32), 32), :] = acc.astype(bf16)
        return 0

    lax.fori_loop(0, shard // 32, total, 0)

    arrived(DX)
    to_rows(got.at[DX], rows_tmp)
    home = home0 + home1

    def collect(n, _):
        tgrad_ref[:, cols(n)] = jnp.dot(
            home, rows_tmp[:, cols(n)], preferred_element_type=f32
        ).astype(bf16)
        return 0

    lax.fori_loop(0, width // WIDE, collect, 0)

    for ph in range(4):
        drained(ph)
    for kind, src, full in stages:
        own3, on4 = pl.ds(0, 3 * shard), pl.ds(0, 4 * shard)
        pltpu.make_async_remote_copy(
            full.at[own3], full.at[own3], w_send.at[kind], w_recv.at[kind, dp],
            device_id=(partner, e), device_id_type=MESH,
        ).wait_send()
        pltpu.make_async_remote_copy(
            full.at[on4], full.at[on4], w_pass.at[kind], w_recv.at[kind, dp],
            device_id=(partner, e), device_id_type=MESH,
        ).wait_send()
    pltpu.make_async_remote_copy(
        part.at[others], parts.at[others], p_send, p_recv, device_id=(partner, e), device_id_type=MESH
    ).wait_send()


def per_device(tokens, out_grad, route_gates, route_slot, gate_weight, up_weight, down_weight):
    tok_dev, width = tokens.shape
    top = route_slot.shape[1]
    n_exp = lax.axis_size("expert")
    n_dp = lax.axis_size("dp")
    cap = max(2, (5 * tok_dev * top + 4 * n_exp - 1) // (4 * n_exp))
    rows = n_exp * cap
    ff = gate_weight.shape[2]
    shard = width // n_dp
    slots = route_slot.reshape(-1)
    order = jnp.arange(slots.shape[0], dtype=jnp.int32)
    earlier = (slots[:, None] == slots[None, :]) & (order[None, :] < order[:, None])
    row_of = slots * cap + jnp.sum(earlier.astype(jnp.int32), axis=1)
    row_of = row_of.reshape(tok_dev, top)

    bf16, f32 = jnp.bfloat16, jnp.float32
    vmem = pl.BlockSpec(memory_space=pltpu.VMEM)
    away = pl.BlockSpec(memory_space=pl.ANY)
    dma = pltpu.SemaphoreType.DMA
    flat = rows * SUB
    moe, tgrad, dgrad = pl.pallas_call(
        functools.partial(layer, cap),
        out_shape=(
            jax.ShapeDtypeStruct((tok_dev, width), bf16),
            jax.ShapeDtypeStruct((tok_dev, width), bf16),
            jax.ShapeDtypeStruct((shard, ff), bf16),
        ),
        in_specs=[vmem] * 6 + [away] * 3,
        out_specs=(vmem, vmem, vmem),
        scratch_shapes=[
            pltpu.VMEM((WIDE, WIDE), bf16),
            pltpu.VMEM((width, ff), bf16),
            pltpu.VMEM((width, ff), bf16),
            pltpu.VMEM((width, ff), bf16),
            pltpu.VMEM((4, flat, LANES), bf16),
            pltpu.VMEM((4, flat, LANES), bf16),
            pltpu.VMEM((4, 2 * cap * SUB, LANES), bf16),
            pltpu.VMEM((rows, width), bf16),
            pltpu.VMEM((rows, width), bf16),
            pltpu.VMEM((rows, width), bf16),
            pltpu.VMEM((rows, ff), f32),
            pltpu.VMEM((rows, ff), f32),
            pltpu.VMEM((rows, ff), bf16),
            pltpu.VMEM((rows, ff), bf16),
            pltpu.VMEM((rows, ff), bf16),
            pltpu.VMEM((width, ff), bf16),
            pltpu.VMEM((width, ff), bf16),
            dma((4,)),
            dma((4,)),
            dma((4,)),
            dma((4,)),
            dma((5,)),
            dma((3,)),
            dma((3,)),
            dma((3,)),
            dma((3, n_dp)),
            dma,
            dma,
        ],
        name="expert_layer",
        compiler_params=pltpu.CompilerParams(
            collective_id=0, has_side_effects=True, vmem_limit_bytes=60 * 1024 * 1024
        ),
    )(
        row_of.T,
        route_gates.T,
        row_of,
        route_gates,
        tokens,
        out_grad,
        gate_weight[0],
        up_weight[0],
        down_weight[0],
    )
    return moe, tgrad, dgrad[None]


def solution(mesh):
    rows = P(("dp", "expert"), None)
    weights = P("expert", "dp", None)
    return jax.shard_map(
        per_device,
        mesh=mesh,
        in_specs=(rows, rows, rows, rows, weights, weights, weights),
        out_specs=(rows, rows, weights),
        check_vma=False,
    )
```

time: 504 us -> 274 us (0.54)
  waiting for transfers between devices: 361 us -> 0 us
  Pallas kernels: 0 us -> 266 us
  starting transfers between devices: 44.1 us -> 0 us
  local copies, waits for them, and re-layouts: 41.6 us -> 7 us
  matrix products: 24.1 us -> 0 us
  other arithmetic: 17.1 us -> 0.2 us
  between operations: 14 us -> 0.69 us
    all_to_all x4 -> x0, waiting for transfers between devices: 359 us -> none  [the longest x1 95.4 us: per_device(): lax.all_to_all(rows_in, 'expert', split_axis=0, concat_axis=0, tiled=True)]
    pallas_call x0 -> x1, Pallas kernels: none -> 266 us  [per_device(): pl.pallas_call(functools.partial(layer, cap), out_shape=(jax.ShapeDtypeSt...]
    all_to_all x4 -> x0, starting transfers between devices: 43.7 us -> none  [the longest x1 18.9 us: per_device(): lax.all_to_all(rows_grad, 'expert', split_axis=0, concat_axis=0, tiled=True)]
    dot_general x7 -> x0, matrix products: 24.1 us -> none  [the longest x1 4.84 us: per_device(): lax.dot_general(grad_flat, hidden_saved, (((0,), (0,)), ((), ())), prefer...]
    gather x7 -> x0, local copies, waits for them, and re-layouts: 16.5 us -> none  [the longest x2 6.4 us: per_device(): tokens[token_row]]
    reshape x7 -> x0, local copies, waits for them, and re-layouts: 14.3 us -> none  [the longest x1 3.38 us: per_device(): outputs.reshape(item_shape)]
    reduce_sum x3 -> x1, other arithmetic: 8.6 us -> 0.18 us  [per_device(): row_of = slots * cap + jnp.sum(earlier.astype(jnp.int32), axis=1)]
  transfers between devices with their start and end apart: 8 -> 0, of which waited for: 4 -> 0; matrix products, arithmetic and copies ran while one was open for 14% -> 0% of each run, Pallas kernels for 0% -> 0%
where the time goes in v2:
time: 274 us
  Pallas kernels  266 us (97%)
  local copies, waits for them, and re-layouts  7 us (3%)
    pallas_call x1, Pallas kernels, per_device(): pl.pallas_call(functools.partial(layer, cap), out_shape=(jax.ShapeDtypeSt...  266 us
    unnamed x15, local copies, waits for them, and re-layouts  5.97 us

profile of v2, /device:TPU:6, one launch (start us, length us, event | category | flops | bytes accessed | tf_op | source)
XLA Modules:
  0.0 274.1 jit_solution(8279126169356120422)
XLA Ops:
  0.6 0.0 copy-start.4
  0.6 0.7 copy-done.4
  1.3 0.0 copy-start.3
  1.3 0.1 copy.25
  1.4 0.6 copy-done.3
  2.0 0.7 copy.27.gate_of_col_ref
  2.7 0.1 copy.24
  2.8 0.1 eq.15
  3.0 0.2 convert_reduce_fusion
  3.2 0.1 reduce_sum.12
  3.3 0.0 copy-start
  3.4 0.6 copy.26.row_of_ref
  4.0 0.0 copy-done
  4.0 266.2 %expert_layer.1 = (bf16[128,2048]{1,0:T(8,128)(2,1)}, bf16[128,2048]{1,0:T(8,128)(2,1)}, bf16[256,768]{1,0:T(8,128)(2,1)}) custom-call(s32[2,128]{1,0:T(2,128)} %copy.26.row_of_ref, f32[2,128]{1,0:T(2,128)} %bitcast.11, s32[128,2]{1,0:T(8,128)} %copy-done, f32[128,2]{1,0:T(8,128)} %copy.27.gate_of_col_ref, bf16[128,2048]{1,0:T(8,128)(2,1)} %tokens_ref.1, ...), custom_call_target="tpu_custom_call" | custom-call | tf_op jit(solution)/shard_map/expert_layer/pallas_call | solution.py:468
  270.2 0.0 copy-start.1
  270.2 1.9 copy.31
  272.2 0.0 copy-done.1
  272.2 0.0 copy-start.2
  272.2 0.8 copy.32
  273.0 0.4 copy-done.2
  273.4 0.7 copy.33
  (2 shorter events, 0.0 us)
Async XLA Ops:
  0.6 0.7 copy-start.4
  1.3 0.7 copy-start.3
  3.3 0.7 copy-start
  270.2 2.0 copy-start.1
  272.2 1.2 copy-start.2

commit v3 on v2

--- a/solution.py
+++ b/solution.py
@@ -10,7 +10,6 @@
 LANES = 128
 SUB = 16
 NX, NY, NZ = 4, 4, 16
-BACK = NZ - 1
 WIDE = 256
 MESH = pl.DeviceIdType.MESH
 X, DY, Y, DX = range(4)
@@ -36,7 +35,6 @@
     w_down,
     sent,
     got,
-    relay,
     rows_x,
     rows_dy,
     rows_tmp,
@@ -49,8 +47,6 @@
     parts,
     send_sem,
     recv_sem,
-    relay_sem,
-    pass_sem,
     own_sem,
     w_own,
     w_send,
@@ -144,51 +140,18 @@
         ).start()
 
     def exchange(ph):
-        far = (z + NZ // 2) % NZ
-        for a in (2, 3):
-            pltpu.make_async_remote_copy(
-                sent.at[ph, block((y + a) % NY * NZ + far)],
-                relay.at[ph, pl.ds((a - 2) * unit, unit)],
-                send_sem.at[ph],
-                relay_sem.at[ph],
-                device_id=(dp, y * NZ + (z + BACK) % NZ),
-                device_id_type=MESH,
-            ).start()
         pltpu.make_async_copy(
             sent.at[ph, block(e)], got.at[ph, block(e)], own_sem.at[ph]
         ).start()
-        for a in (0, 1):
-            send(ph, (y + a) % NY * NZ + far)
+        for a in range(1, NY):
+            send(ph, (y + a) % NY * NZ + z)
 
         def step(i, _):
             for a in range(NY):
                 send(ph, (y + a) % NY * NZ + (z + i) % NZ)
-                send(ph, (y + a) % NY * NZ + (z + NZ // 2 + i) % NZ)
             return 0
 
-        lax.fori_loop(1, NZ // 2, step, 0)
-        for a in range(1, NY):
-            send(ph, (y + a) % NY * NZ + z)
-
-    def pass_on(ph):
-        came = (z + NZ - BACK) % NZ
-        pltpu.make_async_remote_copy(
-            relay.at[ph],
-            relay.at[ph],
-            pass_sem.at[ph],
-            relay_sem.at[ph],
-            device_id=(dp, y * NZ + came),
-            device_id_type=MESH,
-        ).wait_recv()
-        for a in (2, 3):
-            pltpu.make_async_remote_copy(
-                relay.at[ph, pl.ds((a - 2) * unit, unit)],
-                got.at[ph, block(y * NZ + came)],
-                pass_sem.at[ph],
-                recv_sem.at[ph],
-                device_id=(dp, (y + a) % NY * NZ + (came + NZ // 2) % NZ),
-                device_id_type=MESH,
-            ).start()
+        lax.fori_loop(1, NZ, step, 0)
 
     next_e = y * NZ + (z + 1) % NZ
 
@@ -213,14 +176,6 @@
             got.at[ph, most],
             send_sem.at[ph],
             recv_sem.at[ph],
-            device_id=(dp, next_e),
-            device_id_type=MESH,
-        ).wait_send()
-        pltpu.make_async_remote_copy(
-            relay.at[ph],
-            relay.at[ph],
-            pass_sem.at[ph],
-            relay_sem.at[ph],
             device_id=(dp, next_e),
             device_id_type=MESH,
         ).wait_send()
@@ -260,7 +215,6 @@
             ).start()
 
     exchange(X)
-    pass_on(X)
 
     def weight_in(kind, full, owner):
         pltpu.make_async_remote_copy(
@@ -281,6 +235,21 @@
             device_id=(peer, e),
             device_id_type=MESH,
         ).start()
+
+    share = jnp.sum(
+        jnp.where(hit0, gate_of_ref[0:1, :], 0.0) + jnp.where(hit1, gate_of_ref[1:2, :], 0.0),
+        axis=1,
+        keepdims=True,
+    )
+
+    def gather_dy(n, _):
+        taken = jnp.dot(pick, grads_ref[:, cols(n)], preferred_element_type=f32)
+        rows_tmp[:, cols(n)] = (share * taken).astype(bf16)
+        return 0
+
+    lax.fori_loop(0, width // WIDE, gather_dy, 0)
+    to_tiles(rows_tmp, sent.at[DY])
+    exchange(DY)
 
     for kind, _, full in stages:
         weight_in(kind, full, behind)
@@ -288,21 +257,6 @@
         weight_on(kind, full, behind, partner)
         weight_in(kind, full, ahead)
         weight_on(kind, full, ahead, partner)
-
-    share = jnp.sum(
-        jnp.where(hit0, gate_of_ref[0:1, :], 0.0) + jnp.where(hit1, gate_of_ref[1:2, :], 0.0),
-        axis=1,
-        keepdims=True,
-    )
-
-    def gather_dy(n, _):
-        taken = jnp.dot(pick, grads_ref[:, cols(n)], preferred_element_type=f32)
-        rows_tmp[:, cols(n)] = (share * taken).astype(bf16)
-        return 0
-
-    lax.fori_loop(0, width // WIDE, gather_dy, 0)
-    to_tiles(rows_tmp, sent.at[DY])
-    exchange(DY)
 
     for kind, _, full in stages:
         weight_in(kind, full, across)
@@ -336,7 +290,6 @@
 
     lax.fori_loop(0, width // WIDE, project, 0)
     to_tiles(rows_tmp, sent.at[Y])
-    pass_on(DY)
     exchange(Y)
 
     arrived(DY)
@@ -359,7 +312,6 @@
 
     lax.fori_loop(0, width // WIDE, project_back, 0)
     to_tiles(rows_tmp, sent.at[DX])
-    pass_on(Y)
     exchange(DX)
 
     def outer(n, _):
@@ -397,7 +349,6 @@
         return 0
 
     lax.fori_loop(0, width // WIDE, combine, 0)
-    pass_on(DX)
 
     others = pl.ds(0, (n_dp - 1) * shard)
     pltpu.make_async_remote_copy(
@@ -481,7 +432,6 @@
             pltpu.VMEM((width, ff), bf16),
             pltpu.VMEM((4, flat, LANES), bf16),
             pltpu.VMEM((4, flat, LANES), bf16),
-            pltpu.VMEM((4, 2 * cap * SUB, LANES), bf16),
             pltpu.VMEM((rows, width), bf16),
             pltpu.VMEM((rows, width), bf16),
             pltpu.VMEM((rows, width), bf16),
@@ -492,8 +442,6 @@
             pltpu.VMEM((rows, ff), bf16),
             pltpu.VMEM((width, ff), bf16),
             pltpu.VMEM((width, ff), bf16),
-            dma((4,)),
-            dma((4,)),
             dma((4,)),
             dma((4,)),
             dma((5,)),

time: 274 us -> 259 us (0.945)
  Pallas kernels: 266 us -> 251 us
    pallas_call x1, Pallas kernels: 266 us -> 251 us  [per_device(): pl.pallas_call(functools.partial(layer, cap), out_shape=(jax.ShapeDtypeSt...]
where the time goes in v3:
time: 259 us
  Pallas kernels  251 us (97%)
  local copies, waits for them, and re-layouts  7 us (3%)
    pallas_call x1, Pallas kernels, per_device(): pl.pallas_call(functools.partial(layer, cap), out_shape=(jax.ShapeDtypeSt...  251 us
    unnamed x15, local copies, waits for them, and re-layouts  5.97 us

profile of v3, /device:TPU:6, one launch (start us, length us, event | category | flops | bytes accessed | tf_op | source)
XLA Modules:
  0.0 258.9 jit_solution(10826104432055380428)
XLA Ops:
  0.6 0.0 copy-start.4
  0.6 0.7 copy-done.4
  1.3 0.0 copy-start.3
  1.3 0.1 copy.25
  1.4 0.6 copy-done.3
  2.0 0.7 copy.27.gate_of_col_ref
  2.7 0.1 copy.24
  2.8 0.1 eq.15
  3.0 0.2 convert_reduce_fusion
  3.2 0.1 reduce_sum.12
  3.3 0.0 copy-start
  3.4 0.6 copy.26.row_of_ref
  4.0 0.0 copy-done
  4.0 251.1 %expert_layer.1 = (bf16[128,2048]{1,0:T(8,128)(2,1)}, bf16[128,2048]{1,0:T(8,128)(2,1)}, bf16[256,768]{1,0:T(8,128)(2,1)}) custom-call(s32[2,128]{1,0:T(2,128)} %copy.26.row_of_ref, f32[2,128]{1,0:T(2,128)} %bitcast.11, s32[128,2]{1,0:T(8,128)} %copy-done, f32[128,2]{1,0:T(8,128)} %copy.27.gate_of_col_ref, bf16[128,2048]{1,0:T(8,128)(2,1)} %tokens_ref.1, ...), custom_call_target="tpu_custom_call" | custom-call | tf_op jit(solution)/shard_map/expert_layer/pallas_call | solution.py:419
  255.1 0.0 copy-start.1
  255.1 1.9 copy.31
  257.0 0.0 copy-done.1
  257.0 0.0 copy-start.2
  257.0 0.8 copy.32
  257.8 0.4 copy-done.2
  258.2 0.7 copy.33
  (2 shorter events, 0.0 us)
Async XLA Ops:
  0.6 0.7 copy-start.4
  1.3 0.7 copy-start.3
  3.3 0.7 copy-start
  255.1 2.0 copy-start.1
  257.0 1.2 copy-start.2

commit v4 on v3

--- a/solution.py
+++ b/solution.py
@@ -17,10 +17,8 @@
 
 def layer(
     cap,
-    row_of_ref,
-    gate_of_ref,
-    row_of_col_ref,
-    gate_of_col_ref,
+    slots_ref,
+    gates_ref,
     tokens_ref,
     grads_ref,
     gate_in,
@@ -180,9 +178,28 @@
             device_id_type=MESH,
         ).wait_send()
 
-    slot_row = lax.broadcasted_iota(jnp.int32, (rows, tokens_ref.shape[0]), 0)
-    hit0 = slot_row == row_of_ref[0:1, :]
-    hit1 = slot_row == row_of_ref[1:2, :]
+    tok = tokens_ref.shape[0]
+    down_to = lax.broadcasted_iota(jnp.int32, (tok, tok), 0)
+    across_to = lax.broadcasted_iota(jnp.int32, (tok, tok), 1)
+
+    def column(line):
+        return jnp.sum(
+            jnp.where(down_to == across_to, line, jnp.zeros_like(line)), axis=1, keepdims=True
+        )
+
+    lines = [slots_ref[k : k + 1, :] for k in range(2)]
+    columns = [column(line) for line in lines]
+    row_of = []
+    for line in lines:
+        same = (columns[0] == line) | (columns[1] == line)
+        rank = jnp.sum(
+            jnp.where(same & (down_to < across_to), 1, 0).astype(jnp.int32), axis=0, keepdims=True
+        )
+        row_of.append(line * cap + rank)
+
+    slot_row = lax.broadcasted_iota(jnp.int32, (rows, tok), 0)
+    hit0 = slot_row == row_of[0]
+    hit1 = slot_row == row_of[1]
     pick = jnp.where(hit0 | hit1, 1.0, 0.0).astype(bf16)
 
     def gather_x(n, _):
@@ -237,7 +254,7 @@
         ).start()
 
     share = jnp.sum(
-        jnp.where(hit0, gate_of_ref[0:1, :], 0.0) + jnp.where(hit1, gate_of_ref[1:2, :], 0.0),
+        jnp.where(hit0, gates_ref[0:1, :], 0.0) + jnp.where(hit1, gates_ref[1:2, :], 0.0),
         axis=1,
         keepdims=True,
     )
@@ -333,9 +350,11 @@
             device_id_type=MESH,
         ).start()
 
-    token_col = lax.broadcasted_iota(jnp.int32, (tokens_ref.shape[0], rows), 1)
-    home0 = jnp.where(token_col == row_of_col_ref[:, 0:1], 1.0, 0.0).astype(bf16)
-    home1 = jnp.where(token_col == row_of_col_ref[:, 1:2], 1.0, 0.0).astype(bf16)
+    token_col = lax.broadcasted_iota(jnp.int32, (tok, rows), 1)
+    home0 = jnp.where(token_col == column(row_of[0]), 1.0, 0.0).astype(bf16)
+    home1 = jnp.where(token_col == column(row_of[1]), 1.0, 0.0).astype(bf16)
+
+    gate0, gate1 = column(gates_ref[0:1, :]), column(gates_ref[1:2, :])
 
     arrived(Y)
     to_rows(got.at[Y], rows_tmp)
@@ -344,7 +363,7 @@
         first = jnp.dot(home0, rows_tmp[:, cols(n)], preferred_element_type=f32)
         second = jnp.dot(home1, rows_tmp[:, cols(n)], preferred_element_type=f32)
         moe_ref[:, cols(n)] = (
-            gate_of_col_ref[:, 0:1] * first + gate_of_col_ref[:, 1:2] * second
+            gate0 * first + gate1 * second
         ).astype(bf16)
         return 0
 
@@ -405,12 +424,6 @@
     rows = n_exp * cap
     ff = gate_weight.shape[2]
     shard = width // n_dp
-    slots = route_slot.reshape(-1)
-    order = jnp.arange(slots.shape[0], dtype=jnp.int32)
-    earlier = (slots[:, None] == slots[None, :]) & (order[None, :] < order[:, None])
-    row_of = slots * cap + jnp.sum(earlier.astype(jnp.int32), axis=1)
-    row_of = row_of.reshape(tok_dev, top)
-
     bf16, f32 = jnp.bfloat16, jnp.float32
     vmem = pl.BlockSpec(memory_space=pltpu.VMEM)
     away = pl.BlockSpec(memory_space=pl.ANY)
@@ -419,11 +432,11 @@
     moe, tgrad, dgrad = pl.pallas_call(
         functools.partial(layer, cap),
         out_shape=(
-            jax.ShapeDtypeStruct((tok_dev, width), bf16),
-            jax.ShapeDtypeStruct((tok_dev, width), bf16),
-            jax.ShapeDtypeStruct((shard, ff), bf16),
+            pltpu.VMEM((tok_dev, width), bf16),
+            pltpu.VMEM((tok_dev, width), bf16),
+            pltpu.VMEM((shard, ff), bf16),
         ),
-        in_specs=[vmem] * 6 + [away] * 3,
+        in_specs=[vmem] * 4 + [away] * 3,
         out_specs=(vmem, vmem, vmem),
         scratch_shapes=[
             pltpu.VMEM((WIDE, WIDE), bf16),
@@ -457,10 +470,8 @@
             collective_id=0, has_side_effects=True, vmem_limit_bytes=60 * 1024 * 1024
         ),
     )(
-        row_of.T,
+        route_slot.T,
         route_gates.T,
-        row_of,
-        route_gates,
         tokens,
         out_grad,
         gate_weight[0],

time: 259 us -> 253 us (0.977)
  local copies, waits for them, and re-layouts: 7 us -> 2.33 us
    unnamed x15 -> x3, local copies, waits for them, and re-layouts: 5.97 us -> 2.33 us
where the time goes in v4:
time: 253 us
  Pallas kernels  250 us (99%)
    pallas_call x1, Pallas kernels, per_device(): pl.pallas_call(functools.partial(layer, cap), out_shape=(pltpu.VMEM((tok_...  250 us

profile of v4, /device:TPU:6, one launch (start us, length us, event | category | flops | bytes accessed | tf_op | source)
XLA Modules:
  0.0 252.8 jit_solution(15544908916906979542)
XLA Ops:
  0.6 249.8 %expert_layer.1 = (bf16[128,2048]{1,0:T(8,128)(2,1)S(1)}, bf16[128,2048]{1,0:T(8,128)(2,1)S(1)}, bf16[256,768]{1,0:T(8,128)(2,1)S(1)}) custom-call(s32[2,128]{1,0:T(2,128)} %bitcast.10, f32[2,128]{1,0:T(2,128)} %bitcast.11, bf16[128,2048]{1,0:T(8,128)(2,1)} %tokens_ref.1, bf16[128,2048]{1,0:T(8,128)(2,1)} %grads_ref.1, bf16[256,768]{1,0:T(8,128)(2,1)} %bitcast.7, ...), custom_call_target="tpu_custom_call" | custom-call | tf_op jit(solution)/shard_map/expert_layer/pallas_call | solution.py:432
  250.5 0.8 copy.13
  251.3 0.7 copy.15
  252.0 0.8 copy.14

commit v5 on v4

--- a/solution.py
+++ b/solution.py
@@ -52,6 +52,7 @@
     w_recv,
     p_send,
     p_recv,
+    near,
 ):
     f32, bf16 = jnp.float32, jnp.bfloat16
     dp, e = lax.axis_index("dp"), lax.axis_index("expert")
@@ -66,15 +67,24 @@
 
     barrier = pltpu.get_barrier_semaphore()
 
-    def greet(k, _):
+    above = y * NZ + (z + 1) % NZ
+    below = y * NZ + (z + NZ - 1) % NZ
+    for a in range(1, NY):
         pl.semaphore_signal(
-            barrier, inc=1, device_id=(dp, (e + k) % n_exp), device_id_type=MESH
+            barrier, inc=1, device_id=(dp, (y + a) % NY * NZ + z), device_id_type=MESH
         )
-        return 0
-
-    lax.fori_loop(1, n_exp, greet, 0)
+    for p in (above, below):
+        pl.semaphore_signal(barrier, inc=1, device_id=(dp, p), device_id_type=MESH)
     for k in range(1, n_dp):
         pl.semaphore_signal(barrier, inc=1, device_id=((dp + k) % n_dp, e), device_id_type=MESH)
+
+    def tell():
+        pl.semaphore_signal(near.at[0], inc=1, device_id=(dp, above), device_id_type=MESH)
+        pl.semaphore_signal(near.at[1], inc=1, device_id=(dp, below), device_id_type=MESH)
+
+    def meet():
+        pl.semaphore_wait(near.at[0], 1)
+        pl.semaphore_wait(near.at[1], 1)
 
     def block(p):
         return pl.ds(pl.multiple_of(p * unit, SUB), unit)
@@ -89,7 +99,7 @@
     to = lax.broadcasted_iota(jnp.int32, (WIDE, WIDE), 1)
     perm[...] = jnp.where((at % SUB) * SUB + at // SUB == to, 1.0, 0.0).astype(bf16)
 
-    def to_tiles(nat, flat):
+    def to_tiles(nat, flat, first=0, last=rows // 32, unroll=False):
         def step(g, _):
             halves = []
             for h in range(2):
@@ -107,9 +117,9 @@
                 flat[r, :] = moved[:, h * LANES : (h + 1) * LANES]
             return 0
 
-        lax.fori_loop(0, rows // 32, step, 0)
-
-    def to_rows(flat, nat):
+        lax.fori_loop(first, last, step, 0, unroll=unroll)
+
+    def to_rows(flat, nat, unroll=False):
         def step(g, _):
             halves = [
                 flat[pl.ds(pl.multiple_of(g * 512 + h * WIDE, WIDE), WIDE), :] for h in range(2)
@@ -125,7 +135,7 @@
                     ]
             return 0
 
-        lax.fori_loop(0, rows // 32, step, 0)
+        lax.fori_loop(0, rows // 32, step, 0, unroll=unroll)
 
     def send(ph, p):
         pltpu.make_async_remote_copy(
@@ -208,10 +218,17 @@
         ).astype(bf16)
         return 0
 
-    lax.fori_loop(0, width // WIDE, gather_x, 0)
-    to_tiles(rows_tmp, sent.at[X])
-
-    pl.semaphore_wait(barrier, n_exp - 1 + n_dp - 1)
+    pl.semaphore_wait(barrier, NY - 1 + 2 + n_dp - 1)
+    tell()
+    lax.fori_loop(0, width // WIDE, gather_x, 0, unroll=True)
+    meet()
+    tell()
+    to_tiles(rows_tmp, sent.at[X], 0, rows // 64, True)
+    meet()
+    tell()
+    to_tiles(rows_tmp, sent.at[X], rows // 64, rows // 32, True)
+    meet()
+    tell()
 
     turn = 1 - 2 * core
     partner = chip * 2 + 1 - core
@@ -231,7 +248,18 @@
                 device_id_type=MESH,
             ).start()
 
-    exchange(X)
+    pltpu.make_async_copy(sent.at[X, block(e)], got.at[X, block(e)], own_sem.at[X]).start()
+    for a in range(1, NY):
+        send(X, (y + a) % NY * NZ + z)
+    for k in range(1, NZ // 2 + 1):
+        if k > 3:
+            meet()
+            if k < NZ // 2:
+                tell()
+        for a in range(NY):
+            send(X, (y + a) % NY * NZ + (z + k) % NZ)
+            if k < NZ // 2:
+                send(X, (y + a) % NY * NZ + (z + NZ - k) % NZ)
 
     def weight_in(kind, full, owner):
         pltpu.make_async_remote_copy(
@@ -387,7 +415,7 @@
     lax.fori_loop(0, shard // 32, total, 0)
 
     arrived(DX)
-    to_rows(got.at[DX], rows_tmp)
+    to_rows(got.at[DX], rows_tmp, True)
     home = home0 + home1
 
     def collect(n, _):
@@ -396,7 +424,7 @@
         ).astype(bf16)
         return 0
 
-    lax.fori_loop(0, width // WIDE, collect, 0)
+    lax.fori_loop(0, width // WIDE, collect, 0, unroll=True)
 
     for ph in range(4):
         drained(ph)
@@ -413,6 +441,27 @@
     pltpu.make_async_remote_copy(
         part.at[others], parts.at[others], p_send, p_recv, device_id=(partner, e), device_id_type=MESH
     ).wait_send()
+
+
+def put(*refs):
+    n = len(refs) // 2
+    copies = [pltpu.make_async_copy(refs[i], refs[n + i], refs[2 * n].at[i]) for i in range(n)]
+    for copy in copies:
+        copy.start()
+    for copy in copies:
+        copy.wait()
+
+
+def put_out(*arrays):
+    n = len(arrays)
+    return pl.pallas_call(
+        put,
+        out_shape=[jax.ShapeDtypeStruct(a.shape, a.dtype) for a in arrays],
+        in_specs=[pl.BlockSpec(memory_space=pltpu.VMEM)] * n,
+        out_specs=[pl.BlockSpec(memory_space=pl.ANY)] * n,
+        scratch_shapes=[pltpu.SemaphoreType.DMA((n,))],
+        name="put_out",
+    )(*[pltpu.with_memory_space_constraint(a, pltpu.VMEM) for a in arrays])
 
 
 def per_device(tokens, out_grad, route_gates, route_slot, gate_weight, up_weight, down_weight):
@@ -464,6 +513,7 @@
             dma((3, n_dp)),
             dma,
             dma,
+            pltpu.SemaphoreType.REGULAR((2,)),
         ],
         name="expert_layer",
         compiler_params=pltpu.CompilerParams(
@@ -478,6 +528,7 @@
         up_weight[0],
         down_weight[0],
     )
+    moe, tgrad, dgrad = put_out(moe, tgrad, dgrad)
     return moe, tgrad, dgrad[None]
 
 

time: 253 us -> 247 us (0.976)
  Pallas kernels: 250 us -> 246 us
    pallas_call x1, Pallas kernels: 250 us -> 245 us  [per_device(): pl.pallas_call(functools.partial(layer, cap), out_shape=(pltpu.VMEM((tok_...]
where the time goes in v5:
time: 247 us; the launch traced here: 246 us
  Pallas kernels  246 us (100%)
    pallas_call x1, Pallas kernels, per_device(): pl.pallas_call(functools.partial(layer, cap), out_shape=(pltpu.VMEM((tok_...  245 us

profile of v5, /device:TPU:6, one launch (start us, length us, event | category | flops | bytes accessed | tf_op | source)
XLA Modules:
  0.0 246.5 jit_solution(10067605395365786384)
XLA Ops:
  0.6 244.7 %expert_layer.1 = (bf16[128,2048]{1,0:T(8,128)(2,1)S(1)}, bf16[128,2048]{1,0:T(8,128)(2,1)S(1)}, bf16[256,768]{1,0:T(8,128)(2,1)S(1)}) custom-call(s32[2,128]{1,0:T(2,128)} %bitcast.9, f32[2,128]{1,0:T(2,128)} %bitcast.10, bf16[128,2048]{1,0:T(8,128)(2,1)} %tokens_ref.1, bf16[128,2048]{1,0:T(8,128)(2,1)} %grads_ref.1, bf16[256,768]{1,0:T(8,128)(2,1)} %bitcast.6, ...), custom_call_target="tpu_custom_call" | custom-call | tf_op jit(solution)/shard_map/expert_layer/pallas_call | solution.py:481
  245.4 1.1 put_out.1

commit v6 on v5

--- a/solution.py
+++ b/solution.py
@@ -151,15 +151,23 @@
         pltpu.make_async_copy(
             sent.at[ph, block(e)], got.at[ph, block(e)], own_sem.at[ph]
         ).start()
+        def line(dz):
+            for a in range(NY):
+                send(ph, (y + a) % NY * NZ + (z + dz) % NZ)
+
+        def step(i, _):
+            line(7 - i)
+            line(NZ - 2 - i)
+            line(2 + i)
+            line(NZ - 7 + i)
+            return 0
+
+        line(NZ // 2)
+        lax.fori_loop(0, 3, step, 0)
+        line(1)
+        line(NZ - 1)
         for a in range(1, NY):
             send(ph, (y + a) % NY * NZ + z)
-
-        def step(i, _):
-            for a in range(NY):
-                send(ph, (y + a) % NY * NZ + (z + i) % NZ)
-            return 0
-
-        lax.fori_loop(1, NZ, step, 0)
 
     next_e = y * NZ + (z + 1) % NZ
 
@@ -306,10 +314,13 @@
     for kind, _, full in stages:
         weight_in(kind, full, across)
         weight_on(kind, full, across, partner)
-    for kind, src, full in stages:
+    def weights_whole(kind, src, full):
         pltpu.make_async_copy(src, full.at[owner_rows(dp)], w_own.at[kind]).wait()
         for k in range(NX):
             weight_in(kind, full, (chip + k) % NX * 2 + 1 - core)
+
+    for stage in stages[:2]:
+        weights_whole(*stage)
 
     arrived(X)
     to_rows(got.at[X], rows_x)
@@ -326,6 +337,7 @@
 
     lax.fori_loop(0, ff // WIDE, forward, 0)
     across_ff = (((1,), (1,)), ((), ()))
+    weights_whole(*stages[2])
 
     def project(n, _):
         rows_tmp[:, cols(n)] = lax.dot_general(

time: 247 us -> 249 us (level)
  no operation moved by 1% of the time
where the time goes in v6:
time: 249 us; the launch traced here: 248 us
  Pallas kernels  247 us (99%)
    pallas_call x1, Pallas kernels, per_device(): pl.pallas_call(functools.partial(layer, cap), out_shape=(pltpu.VMEM((tok_...  246 us

profile of v6, /device:TPU:6, one launch (start us, length us, event | category | flops | bytes accessed | tf_op | source)
XLA Modules:
  0.0 247.7 jit_solution(3607460871672171311)
XLA Ops:
  0.6 245.9 %expert_layer.1 = (bf16[128,2048]{1,0:T(8,128)(2,1)S(1)}, bf16[128,2048]{1,0:T(8,128)(2,1)S(1)}, bf16[256,768]{1,0:T(8,128)(2,1)S(1)}) custom-call(s32[2,128]{1,0:T(2,128)} %bitcast.9, f32[2,128]{1,0:T(2,128)} %bitcast.10, bf16[128,2048]{1,0:T(8,128)(2,1)} %tokens_ref.1, bf16[128,2048]{1,0:T(8,128)(2,1)} %grads_ref.1, bf16[256,768]{1,0:T(8,128)(2,1)} %bitcast.6, ...), custom_call_target="tpu_custom_call" | custom-call | tf_op jit(solution)/shard_map/expert_layer/pallas_call | solution.py:493
  246.6 1.1 put_out.1

commit v7 on v5

--- a/solution.py
+++ b/solution.py
@@ -43,6 +43,7 @@
     d_up,
     part,
     parts,
+    partial,
     send_sem,
     recv_sem,
     own_sem,
@@ -137,12 +138,13 @@
 
         lax.fori_loop(0, rows // 32, step, 0, unroll=unroll)
 
-    def send(ph, p):
+    def send(ph, p, sem=None):
+        sem = ph if sem is None else sem
         pltpu.make_async_remote_copy(
             sent.at[ph, block(p)],
             got.at[ph, block(e)],
-            send_sem.at[ph],
-            recv_sem.at[ph],
+            send_sem.at[sem],
+            recv_sem.at[sem],
             device_id=(dp, p),
             device_id_type=MESH,
         ).start()
@@ -212,23 +214,46 @@
     hit1 = slot_row == row_of[1]
     pick = jnp.where(hit0 | hit1, 1.0, 0.0).astype(bf16)
 
-    def gather_x(n, _):
-        rows_tmp[:, cols(n)] = jnp.dot(
-            pick, tokens_ref[:, cols(n)], preferred_element_type=f32
-        ).astype(bf16)
-        return 0
+    half = rows // 2
+
+    def gather_x(h):
+        held = pick[h * half : (h + 1) * half]
+
+        def step(n, _):
+            rows_tmp[h * half : (h + 1) * half, cols(n)] = jnp.dot(
+                held, tokens_ref[:, cols(n)], preferred_element_type=f32
+            ).astype(bf16)
+            return 0
+
+        lax.fori_loop(0, width // WIDE, step, 0, unroll=True)
 
     pl.semaphore_wait(barrier, NY - 1 + 2 + n_dp - 1)
     tell()
-    lax.fori_loop(0, width // WIDE, gather_x, 0, unroll=True)
+    def sides(k, lines):
+        for to_y in lines:
+            send(X, to_y * NZ + (z + k) % NZ)
+            if k < NZ // 2:
+                send(X, to_y * NZ + (z + NZ - k) % NZ)
+
+    early, late = range(NY // 2), range(NY // 2, NY)
+    gather_x(0)
     meet()
     tell()
     to_tiles(rows_tmp, sent.at[X], 0, rows // 64, True)
+    sides(1, early)
+    meet()
+    tell()
+    sides(2, early)
+    gather_x(1)
     meet()
     tell()
     to_tiles(rows_tmp, sent.at[X], rows // 64, rows // 32, True)
+    sides(1, late)
+    sides(2, late)
+    sides(3, range(NY))
     meet()
     tell()
+    sides(4, range(NY))
 
     turn = 1 - 2 * core
     partner = chip * 2 + 1 - core
@@ -251,15 +276,11 @@
     pltpu.make_async_copy(sent.at[X, block(e)], got.at[X, block(e)], own_sem.at[X]).start()
     for a in range(1, NY):
         send(X, (y + a) % NY * NZ + z)
-    for k in range(1, NZ // 2 + 1):
-        if k > 3:
-            meet()
-            if k < NZ // 2:
-                tell()
-        for a in range(NY):
-            send(X, (y + a) % NY * NZ + (z + k) % NZ)
-            if k < NZ // 2:
-                send(X, (y + a) % NY * NZ + (z + NZ - k) % NZ)
+    for k in range(5, NZ // 2 + 1):
+        meet()
+        if k < NZ // 2:
+            tell()
+        sides(k, range(NY))
 
     def weight_in(kind, full, owner):
         pltpu.make_async_remote_copy(
@@ -357,7 +378,23 @@
 
     lax.fori_loop(0, width // WIDE, project_back, 0)
     to_tiles(rows_tmp, sent.at[DX])
-    exchange(DX)
+    pair, other = y // 2, 1 - y // 2
+    pltpu.make_async_copy(sent.at[DX, block(e)], got.at[DX, block(e)], own_sem.at[DX]).start()
+    beside = pair * 2 + 1 - y % 2
+
+    def send_near(i, _):
+        for to_y in (y, beside):
+            send(DX, to_y * NZ + (z + i) % NZ)
+        return 0
+
+    def send_other(i, _):
+        for k in range(2):
+            send(DX, (other * 2 + k) * NZ + (z + i) % NZ, 4)
+        return 0
+
+    send(DX, beside * NZ + z)
+    lax.fori_loop(1, NZ, send_near, 0)
+    lax.fori_loop(0, NZ, send_other, 0)
 
     def outer(n, _):
         part[cols(n), :] = lax.dot_general(
@@ -414,19 +451,67 @@
 
     lax.fori_loop(0, shard // 32, total, 0)
 
-    arrived(DX)
-    to_rows(got.at[DX], rows_tmp, True)
-    home = home0 + home1
-
-    def collect(n, _):
-        tgrad_ref[:, cols(n)] = jnp.dot(
-            home, rows_tmp[:, cols(n)], preferred_element_type=f32
+    pair_rows = NZ * 2 * unit
+
+    def half_dx(count, sem):
+        some = pl.ds(0, count * unit)
+        return pltpu.make_async_remote_copy(
+            sent.at[DX, some],
+            got.at[DX, some],
+            send_sem.at[sem],
+            recv_sem.at[sem],
+            device_id=(dp, next_e),
+            device_id_type=MESH,
+        )
+
+    col_half = lax.broadcasted_iota(jnp.int32, (tok, half), 1)
+
+    def home_of(which):
+        at_row = col_half + which * half
+        mine = (at_row == column(row_of[0])) | (at_row == column(row_of[1]))
+        return jnp.where(mine, 1.0, 0.0).astype(bf16)
+
+    def pair_in(which):
+        def step(g, _):
+            halves = [
+                got[
+                    DX,
+                    pl.ds(pl.multiple_of(which * pair_rows + g * 512 + h * WIDE, WIDE), WIDE),
+                    :,
+                ]
+                for h in range(2)
+            ]
+            moved = jnp.dot(
+                perm[...], jnp.concatenate(halves, axis=1), preferred_element_type=f32
+            ).astype(bf16)
+            for h in range(2):
+                for j in range(SUB):
+                    rows_tmp[
+                        g * 32 + h * SUB : g * 32 + (h + 1) * SUB, j * LANES : (j + 1) * LANES
+                    ] = moved[j * SUB : (j + 1) * SUB, h * LANES : (h + 1) * LANES]
+            return 0
+
+        for g in range(rows // 64):
+            step(g, 0)
+
+    home_pair, home_other = home_of(pair), home_of(other)
+    half_dx(NZ * 2 - 1, DX).wait_recv()
+    pltpu.make_async_copy(sent.at[DX, block(e)], got.at[DX, block(e)], own_sem.at[DX]).wait()
+    pair_in(pair)
+    for n in range(width // WIDE):
+        c = slice(n * WIDE, (n + 1) * WIDE)
+        partial[:, c] = jnp.dot(home_pair, rows_tmp[0:half, c], preferred_element_type=f32)
+    half_dx(NZ * 2, 4).wait_recv()
+    pair_in(other)
+    for n in range(width // WIDE):
+        c = slice(n * WIDE, (n + 1) * WIDE)
+        tgrad_ref[:, c] = (
+            partial[:, c] + jnp.dot(home_other, rows_tmp[0:half, c], preferred_element_type=f32)
         ).astype(bf16)
-        return 0
-
-    lax.fori_loop(0, width // WIDE, collect, 0, unroll=True)
-
-    for ph in range(4):
+
+    half_dx(NZ * 2 - 1, DX).wait_send()
+    half_dx(NZ * 2, 4).wait_send()
+    for ph in range(3):
         drained(ph)
     for kind, src, full in stages:
         own3, on4 = pl.ds(0, 3 * shard), pl.ds(0, 4 * shard)
@@ -504,8 +589,9 @@
             pltpu.VMEM((rows, ff), bf16),
             pltpu.VMEM((width, ff), bf16),
             pltpu.VMEM((width, ff), bf16),
-            dma((4,)),
-            dma((4,)),
+            pltpu.VMEM((tok_dev, width), f32),
+            dma((5,)),
+            dma((5,)),
             dma((5,)),
             dma((3,)),
             dma((3,)),

time: 247 us -> 248 us (level)
  no operation moved by 1% of the time
where the time goes in v7:
time: 248 us; the launch traced here: 246 us
  Pallas kernels  245 us (99%)
    pallas_call x1, Pallas kernels, per_device(): pl.pallas_call(functools.partial(layer, cap), out_shape=(pltpu.VMEM((tok_...  244 us

profile of v7, /device:TPU:6, one launch (start us, length us, event | category | flops | bytes accessed | tf_op | source)
XLA Modules:
  0.0 245.7 jit_solution(7989872413577756474)
XLA Ops:
  0.6 244.0 %expert_layer.1 = (bf16[128,2048]{1,0:T(8,128)(2,1)S(1)}, bf16[128,2048]{1,0:T(8,128)(2,1)S(1)}, bf16[256,768]{1,0:T(8,128)(2,1)S(1)}) custom-call(s32[2,128]{1,0:T(2,128)} %bitcast.9, f32[2,128]{1,0:T(2,128)} %bitcast.10, bf16[128,2048]{1,0:T(8,128)(2,1)} %tokens_ref.1, bf16[128,2048]{1,0:T(8,128)(2,1)} %grads_ref.1, bf16[256,768]{1,0:T(8,128)(2,1)} %bitcast.6, ...), custom_call_target="tpu_custom_call" | custom-call | tf_op jit(solution)/shard_map/expert_layer/pallas_call | solution.py:566
  244.6 1.1 put_out.1

commit v8 on v5

--- a/solution.py
+++ b/solution.py
@@ -236,6 +236,14 @@
     behind = (chip + NX - turn) % NX * 2 + core
     across = (chip + 2) % NX * 2 + core
     stages = ((0, gate_in, w_gate), (1, up_in, w_up), (2, down_in, w_down))
+    pltpu.make_async_copy(sent.at[X, block(e)], got.at[X, block(e)], own_sem.at[X]).start()
+    for a in range(1, NY):
+        send(X, (y + a) % NY * NZ + z)
+    for k in range(1, 4):
+        for a in range(NY):
+            send(X, (y + a) % NY * NZ + (z + k) % NZ)
+            send(X, (y + a) % NY * NZ + (z + NZ - k) % NZ)
+
     for kind, src, full in stages:
         pltpu.make_async_copy(src, full.at[owner_rows(dp)], w_own.at[kind]).start()
         for peer in (ahead, behind, partner):
@@ -248,14 +256,10 @@
                 device_id_type=MESH,
             ).start()
 
-    pltpu.make_async_copy(sent.at[X, block(e)], got.at[X, block(e)], own_sem.at[X]).start()
-    for a in range(1, NY):
-        send(X, (y + a) % NY * NZ + z)
-    for k in range(1, NZ // 2 + 1):
-        if k > 3:
-            meet()
-            if k < NZ // 2:
-                tell()
+    for k in range(4, NZ // 2 + 1):
+        meet()
+        if k < NZ // 2:
+            tell()
         for a in range(NY):
             send(X, (y + a) % NY * NZ + (z + k) % NZ)
             if k < NZ // 2:

time: 247 us -> 247 us (level)
  no operation moved by 1% of the time
where the time goes in v8:
time: 247 us; the launch traced here: 246 us
  Pallas kernels  246 us (100%)
    pallas_call x1, Pallas kernels, per_device(): pl.pallas_call(functools.partial(layer, cap), out_shape=(pltpu.VMEM((tok_...  245 us

profile of v8, /device:TPU:6, one launch (start us, length us, event | category | flops | bytes accessed | tf_op | source)
XLA Modules:
  0.0 246.4 jit_solution(6872759489475338704)
XLA Ops:
  0.6 244.7 %expert_layer.1 = (bf16[128,2048]{1,0:T(8,128)(2,1)S(1)}, bf16[128,2048]{1,0:T(8,128)(2,1)S(1)}, bf16[256,768]{1,0:T(8,128)(2,1)S(1)}) custom-call(s32[2,128]{1,0:T(2,128)} %bitcast.9, f32[2,128]{1,0:T(2,128)} %bitcast.10, bf16[128,2048]{1,0:T(8,128)(2,1)} %tokens_ref.1, bf16[128,2048]{1,0:T(8,128)(2,1)} %grads_ref.1, bf16[256,768]{1,0:T(8,128)(2,1)} %bitcast.6, ...), custom_call_target="tpu_custom_call" | custom-call | tf_op jit(solution)/shard_map/expert_layer/pallas_call | solution.py:485
  245.3 1.1 put_out.1
